TPU v7x, 256 devices: a whole 4x4x8 slice. The times are simulated.
256 devices in a mesh: samp: 32 (over z_hi, y, x), feat: 8 (over z_lo, core).
Axes of the slice: x: 4, y: 4, z: 8 (z_hi: 2, z_lo: 4; z = z_hi * 4 + z_lo), core: 2. Of those that a mesh axis runs over, the one named last changes fastest.
Arguments:
- counters: bfloat16 [32768, 512], P('samp'), may hold values from -6 to 6
- frequencies: bfloat16 [512, 4096], P(None, 'feat'), may hold values from -0.25 to 0.25
- phases: bfloat16 [1, 4096], P(None, 'feat'), may hold values from -3.140625 to 3.140625
- targets: bfloat16 [32768, 64], P('samp'), may hold values from -6 to 6
Outputs:
- solution: float32 [4096, 64], P('samp')
- residual: float32 [4096, 64], P('samp')
- gram: float32 [4096, 4096], P('samp', 'feat')
All inputs are finite; a program needn't handle non-finite values.
Results may differ from a plain program's by a relative error of at most 0.0035.
Values may be sent and summed in bfloat16 or wider, within the bound.
A program may use at most 64 MiB of HBM per device.

v0:
```python
import math
import jax
import jax.numpy as jnp
from jax import lax
from jax.sharding import PartitionSpec as P

ITERS = 2
RIDGE = 0.05


def on_device(counters, frequencies, phases, targets):
    rows = counters.shape[0]
    block_width = frequencies.shape[1]
    mixed = jnp.dot(counters, frequencies, preferred_element_type=jnp.float32)
    local_feats = jnp.cos(mixed + phases.astype(jnp.float32)).astype(jnp.bfloat16)
    features_all = lax.all_gather(local_feats, "feat", axis=1, tiled=True)
    joined = jnp.concatenate([local_feats, targets], axis=1)
    inner = (((0,), (0,)), ((), ()))
    reduced = lax.psum_scatter(
        lax.dot_general(features_all, joined, inner, preferred_element_type=jnp.float32),
        "samp",
        scatter_dimension=0,
        tiled=True,
    )
    samples = rows * lax.axis_size("samp")
    gram_block = reduced[:, :block_width] / samples
    right_side = reduced[:, block_width:] / math.sqrt(samples)
    feat_offset = lax.axis_index("feat") * block_width

    def squares(vector):
        return lax.psum(jnp.sum(vector * vector, axis=0), "samp")

    solution = jnp.zeros_like(right_side)
    residual = right_side
    direction = right_side
    norm_now = squares(residual)
    for iteration in range(ITERS):
        gathered = lax.all_gather(direction, "samp", axis=0, tiled=True)
        selected = lax.dynamic_slice_in_dim(gathered, feat_offset, block_width, 0)
        partial_value = jnp.dot(gram_block, selected, precision=lax.Precision.HIGHEST)
        image = lax.psum(partial_value, "feat") + RIDGE * direction
        curve = lax.psum(jnp.sum(direction * image, axis=0), "samp")
        step_size = norm_now / curve
        solution = solution + step_size * direction
        residual = residual - step_size * image
        norm_next = squares(residual)
        direction = residual + norm_next / norm_now * direction
        norm_now = norm_next
    return (solution, residual, gram_block)


def solution(mesh):
    return jax.shard_map(
        on_device,
        mesh=mesh,
        in_specs=(P("samp", None), P(None, "feat"), P(None, "feat"), P("samp", None)),
        out_specs=(P("samp", None), P("samp", None), P("samp", "feat")),
        check_vma=False,
    )
```

profile of v0, /device:TPU:128, one launch (start us, length us, event | category | flops | bytes accessed | tf_op | source)
XLA Modules:
  0.0 973.0 jit_solution(9429398603258121843)
XLA Ops:
  7.2 0.8 add.52
  8.0 0.4 copy-done
  8.4 9.2 cosine_convert_fusion
  17.7 93.0 %all-gather.4.cloned.1.call-done = bf16[1024,4096]{0,1:T(8,128)(2,1)} async-done(((bf16[1024,512]{0,1:T(8,128)(2,1)}), bf16[1024,4096]{0,1:T(8,128)(2,1)}) %all-gather.4.cloned.1.call-update) | async-done | bytes 8388624 | tf_op jit(solution)/shard_map/all_gather | solution.py:16
  110.7 9.9 %fusion = f32[4096,576]{0,1:T(8,128)} fusion(bf16[1024,4096]{0,1:T(8,128)(2,1)} %all-gather.4.cloned.1.call-done, bf16[1024,64]{0,1:T(8,128)(2,1)S(1)} %copy-done.1, bf16[1024,512]{0,1:T(8,128)(2,1)} %cosine_convert_fusion), kind=kOutput, calls=%fused_computation.1 | convolution fusion | flops 4834197504 | bytes 19005440 | tf_op jit(solution)/shard_map/dot_general | solution.py:20
  120.6 0.0 all-gather.6.cloned.1.call-start
  120.7 283.7 %reduce-scatter.2.cloned.1.call-done = f32[128,576]{0,1:T(8,128)} async-done(((f32[4096,576]{0,1:T(8,128)}), f32[128,576]{0,1:T(8,128)}) %reduce-scatter.2.cloned.1.call-update) | async-done | bytes 294928 | tf_op jit(solution)/shard_map/reduce_scatter | solution.py:19
  404.4 1.4 slice_multiply_fusion.1
  405.8 79.4 %all-gather.6.cloned.1.call-done = f32[4096,64]{0,1:T(8,128)} async-done(((f32[128,64]{0,1:T(8,128)}), f32[4096,64]{0,1:T(8,128)}) %all-gather.6.cloned.1.call-update) | async-done | bytes 1048592 | tf_op jit(solution)/shard_map/all_gather | solution.py:38
  485.2 1.3 fusion.6
  486.5 29.9 %psum.43 = f32[128,64]{0,1:T(8,128)S(1)} all-reduce(f32[128,64]{0,1:T(8,128)S(1)} %fusion.6), channel_id=1, replica_groups=mesh['samp'=32,'feat'=8] {'feat'}, use_global_device_ids=true, to_apply=%region_3.0 | all-reduce | flops 8192 | bytes 65536 | tf_op jit(solution)/shard_map/psum | solution.py:41
  516.4 0.9 multiply_reduce_fusion.2
  517.3 115.8 %all-reduce = (f32[64]{0:T(128)S(1)}, f32[64]{0:T(128)S(1)}) all-reduce(f32[64]{0:T(128)S(1)} %get-tuple-element.7, f32[64]{0:T(128)S(1)} %get-tuple-element.6), channel_id=1, replica_groups=mesh['samp'=32,'feat'=8] {'samp'}, use_global_device_ids=true, to_apply=%region_2.0 | all-reduce | flops 128 | bytes 1024 | tf_op jit(solution)/shard_map/psum | solution.py:31
  633.1 0.9 multiply_reduce_fusion.1
  634.0 108.1 %psum.45 = f32[64]{0:T(128)S(1)} all-reduce(f32[64]{0:T(128)S(1)} %get-tuple-element.12), channel_id=1, replica_groups=mesh['samp'=32,'feat'=8] {'samp'}, use_global_device_ids=true, to_apply=%region_7.0 | all-reduce | flops 64 | bytes 512 | tf_op jit(solution)/shard_map/psum | solution.py:31
  742.1 1.5 multiply_add_fusion.2
  743.6 1.0 slice_multiply_fusion
  744.6 0.8 copy.7
  745.4 71.7 %all-gather.8.cloned.1.call-done = f32[4096,64]{0,1:T(8,128)} async-done(((f32[128,64]{0,1:T(8,128)}), f32[4096,64]{0,1:T(8,128)}) %all-gather.8.cloned.1.call-update) | async-done | bytes 1048592 | tf_op jit(solution)/shard_map/all_gather | solution.py:38
  817.1 1.3 fusion.4
  818.4 29.9 %psum.46 = f32[128,64]{0,1:T(8,128)S(1)} all-reduce(f32[128,64]{0,1:T(8,128)S(1)} %fusion.4), channel_id=1, replica_groups=mesh['samp'=32,'feat'=8] {'feat'}, use_global_device_ids=true, to_apply=%region_8.0 | all-reduce | flops 8192 | bytes 65536 | tf_op jit(solution)/shard_map/psum | solution.py:41
  848.3 0.9 multiply_reduce_fusion
  849.2 115.8 %psum.47 = f32[64]{0:T(128)S(1)} all-reduce(f32[64]{0:T(128)S(1)} %multiply_reduce_fusion), channel_id=1, replica_groups=mesh['samp'=32,'feat'=8] {'samp'}, use_global_device_ids=true, to_apply=%region_10.0 | all-reduce | flops 64 | bytes 512 | tf_op jit(solution)/shard_map/psum | solution.py:42
  965.0 1.5 multiply_subtract_fusion
  (13 shorter events, 0.2 us)
Async XLA Ops:
  7.2 1.2 copy-start
  7.2 103.5 %all-gather.4.cloned.1.call-start = ((), (), s32[]{:S(2)}) async-start(), calls=%async_computation.1 | async-start | bytes 9437184 | tf_op jit(solution)/shard_map/all_gather | solution.py:16
  8.4 102.2 %copy-start.1 = (bf16[1024,64]{0,1:T(8,128)(2,1)S(1)}, bf16[1024,64]{0,1:T(8,128)(2,1)}, u32[]{:S(2)}) copy-start(bf16[1024,64]{0,1:T(8,128)(2,1)} %param.7) | copy-start | bytes 393220
  17.6 386.7 %reduce-scatter.2.cloned.1.call-start = ((), (), s32[]{:S(2)}) async-start(), calls=%async_computation.2 | async-start | bytes 9732096 | tf_op jit(solution)/shard_map/reduce_scatter | solution.py:19
  120.6 364.6 %all-gather.6.cloned.1.call-start = ((), (), s32[]{:S(2)}) async-start(), calls=%async_computation.3 | async-start | bytes 1081344 | tf_op jit(solution)/shard_map/all_gather | solution.py:38
  405.8 411.4 %all-gather.8.cloned.1.call-start = ((), (), s32[]{:S(2)}) async-start(), calls=%async_computation.4 | async-start | bytes 1081344 | tf_op jit(solution)/shard_map/all_gather | solution.py:38
Sparse Core Ops, SparseCore 0:
  17.8 92.8 all-gather.3
  120.7 283.5 reduce-scatter.1
  408.7 76.5 all-gather.5
  743.7 73.3 all-gather.7
where the time goes:
time: 974 us; the launch traced here: 973 us
  waiting for transfers between devices  528 us (54%)
  blocking collectives  399 us (41%)
  matrix products  21.7 us (2%)
  between operations  13.8 us (1%)
    reduce_scatter x1, waiting for transfers between devices, on_device(): lax.psum_scatter(lax.dot_general(features_all, joined, inner, preferred_e...  284 us
    psum x2, blocking collectives, squares(): return lax.psum(jnp.sum(vector * vector, axis=0), 'samp')  224 us
    all_gather x2, waiting for transfers between devices, on_device(): gathered = lax.all_gather(direction, 'samp', axis=0, tiled=True)  151 us
    psum x1, blocking collectives, on_device(): curve = lax.psum(jnp.sum(direction * image, axis=0), 'samp')  116 us
    all_gather x1, waiting for transfers between devices, on_device(): features_all = lax.all_gather(local_feats, 'feat', axis=1, tiled=True)  93 us
    psum x2, blocking collectives, on_device(): image = lax.psum(partial_value, 'feat') + RIDGE * direction  59.8 us
  transfers between devices with their start and end apart: 4, of which 4 were waited for; matrix products, arithmetic and copies ran while one was open for 0% of the time, Pallas kernels for 0%

commit v1 on v0

--- a/solution.py
+++ b/solution.py
@@ -6,6 +6,12 @@
 
 ITERS = 2
 RIDGE = 0.05
+
+
+def launch_keys(buf):
+    return jnp.concatenate(
+        lax.all_to_all(jnp.stack([buf for _ in range(lax.axis_size("samp"))]), "samp", 0, 0), axis=0
+    )
 
 
 def on_device(counters, frequencies, phases, targets):
@@ -35,7 +41,7 @@
     direction = right_side
     norm_now = squares(residual)
     for iteration in range(ITERS):
-        gathered = lax.all_gather(direction, "samp", axis=0, tiled=True)
+        gathered = launch_keys(direction)
         selected = lax.dynamic_slice_in_dim(gathered, feat_offset, block_width, 0)
         partial_value = jnp.dot(gram_block, selected, precision=lax.Precision.HIGHEST)
         image = lax.psum(partial_value, "feat") + RIDGE * direction

time: 974 us -> 868 us (0.89)
  waiting for transfers between devices: 528 us -> 406 us
  starting transfers between devices: 0.16 us -> 18.7 us
    all_gather x2 -> x0, waiting for transfers between devices: 151 us -> none  [on_device(): gathered = lax.all_gather(direction, 'samp', axis=0, tiled=True)]
    all_to_all x0 -> x2, waiting for transfers between devices: none -> 29.6 us  [launch_keys(): lax.all_to_all(jnp.stack([buf for _ in range(lax.axis_size('samp'))]), 's...]
    all_to_all x0 -> x2, starting transfers between devices: none -> 18.6 us  [launch_keys(): lax.all_to_all(jnp.stack([buf for _ in range(lax.axis_size('samp'))]), 's...]
where the time goes in v1:
time: 868 us; the launch traced here: 863 us
  waiting for transfers between devices  406 us (47%)
  blocking collectives  398 us (46%)
  matrix products  19.8 us (2%)
  starting transfers between devices  18.7 us (2%)
  between operations  14.1 us (2%)
    reduce_scatter x1, waiting for transfers between devices, on_device(): lax.psum_scatter(lax.dot_general(features_all, joined, inner, preferred_e...  284 us
    psum x2, blocking collectives, squares(): return lax.psum(jnp.sum(vector * vector, axis=0), 'samp')  226 us
    psum x1, blocking collectives, on_device(): curve = lax.psum(jnp.sum(direction * image, axis=0), 'samp')  111 us
    all_gather x1, waiting for transfers between devices, on_device(): features_all = lax.all_gather(local_feats, 'feat', axis=1, tiled=True)  93 us
    psum x2, blocking collectives, on_device(): image = lax.psum(partial_value, 'feat') + RIDGE * direction  60.8 us
    all_to_all x2, waiting for transfers between devices, launch_keys(): lax.all_to_all(jnp.stack([buf for _ in range(lax.axis_size('samp'))]), 's...  29.6 us
    all_to_all x2, starting transfers between devices, launch_keys(): lax.all_to_all(jnp.stack([buf for _ in range(lax.axis_size('samp'))]), 's...  18.6 us
  transfers between devices with their start and end apart: 4, of which 4 were waited for; matrix products, arithmetic and copies ran while one was open for 0% of the time, Pallas kernels for 0%

profile of v1, /device:TPU:128, one launch (start us, length us, event | category | flops | bytes accessed | tf_op | source)
XLA Modules:
  0.0 862.9 jit_solution(8468425917946293748)
XLA Ops:
  7.2 0.8 add.52
  8.0 0.4 copy-done
  8.4 9.2 %cosine_convert_fusion = bf16[1024,512]{0,1:T(8,128)(2,1)} fusion(bf16[1024,512]{1,0:T(8,128)(2,1)S(1)} %copy-done, bf16[512,512]{1,0:T(8,128)(2,1)} %param.5, f32[512]{0:T(512)S(1)} %bitcast.14), kind=kOutput, calls=%fused_computation | convolution fusion | flops 537919488 | bytes 2623488 | tf_op jit(solution)/shard_map/dot_general | solution.py:20
  17.7 93.0 %all-gather.2.cloned.1.call-done = bf16[1024,4096]{0,1:T(8,128)(2,1)} async-done(((bf16[1024,512]{0,1:T(8,128)(2,1)}), bf16[1024,4096]{0,1:T(8,128)(2,1)}) %all-gather.2.cloned.1.call-update) | async-done | bytes 8388624 | tf_op jit(solution)/shard_map/all_gather | solution.py:22
  110.7 9.9 %fusion = f32[4096,576]{0,1:T(8,128)} fusion(bf16[1024,4096]{0,1:T(8,128)(2,1)} %all-gather.2.cloned.1.call-done, bf16[1024,64]{0,1:T(8,128)(2,1)S(1)} %copy-done.2, bf16[1024,512]{0,1:T(8,128)(2,1)} %cosine_convert_fusion), kind=kOutput, calls=%fused_computation.1 | convolution fusion | flops 4834197504 | bytes 19005440 | tf_op jit(solution)/shard_map/dot_general | solution.py:26
  120.6 283.7 %reduce-scatter.2.cloned.1.call-done = f32[128,576]{0,1:T(8,128)} async-done(((f32[4096,576]{0,1:T(8,128)}), f32[128,576]{0,1:T(8,128)}) %reduce-scatter.2.cloned.1.call-update) | async-done | bytes 294928 | tf_op jit(solution)/shard_map/reduce_scatter | solution.py:25
  404.4 0.8 slice_multiply_fusion.1
  405.1 1.1 stack.4
  406.2 11.2 %all-to-all-start = ((f32[32,128,64]{1,2,0:T(8,128)}), f32[32,128,64]{1,2,0:T(8,128)S(1)}, u32[]{:S(2)}, u32[]{:S(2)}) async-start(f32[32,128,64]{1,2,0:T(8,128)} %stack.4), calls=%async_computation.1 | async-start | bytes 2097152 | tf_op jit(solution)/shard_map/all_to_all | solution.py:13
  417.5 14.5 %all-to-all-done = f32[32,128,64]{1,2,0:T(8,128)S(1)} async-done(((f32[32,128,64]{1,2,0:T(8,128)}), f32[32,128,64]{1,2,0:T(8,128)S(1)}, u32[]{:S(2)}, u32[]{:S(2)}) %all-to-all-start) | async-done | bytes 1048608 | tf_op jit(solution)/shard_map/all_to_all | solution.py:13
  432.1 0.3 fusion.6
  432.4 34.9 %psum.43 = f32[128,64]{0,1:T(8,128)S(1)} all-reduce(f32[128,64]{0,1:T(8,128)S(1)} %fusion.6), channel_id=1, replica_groups=mesh['samp'=32,'feat'=8] {'feat'}, use_global_device_ids=true, to_apply=%region_3.0 | all-reduce | flops 8192 | bytes 65536 | tf_op jit(solution)/shard_map/psum | solution.py:47
  467.2 0.1 multiply_reduce_fusion.2
  467.4 115.6 %all-reduce = (f32[64]{0:T(128)S(1)}, f32[64]{0:T(128)S(1)}) all-reduce(f32[64]{0:T(128)S(1)} %get-tuple-element.13, f32[64]{0:T(128)S(1)} %get-tuple-element.12), channel_id=1, replica_groups=mesh['samp'=32,'feat'=8] {'samp'}, use_global_device_ids=true, to_apply=%region_2.0 | all-reduce | flops 128 | bytes 1024 | tf_op jit(solution)/shard_map/psum | solution.py:37
  583.0 0.2 multiply_reduce_fusion.1
  583.2 110.5 %psum.45 = f32[64]{0:T(128)S(1)} all-reduce(f32[64]{0:T(128)S(1)} %get-tuple-element.18), channel_id=1, replica_groups=mesh['samp'=32,'feat'=8] {'samp'}, use_global_device_ids=true, to_apply=%region_7.0 | all-reduce | flops 64 | bytes 512 | tf_op jit(solution)/shard_map/psum | solution.py:37
  693.8 1.1 stack.5
  694.9 7.4 all-to-all-start.1
  702.3 0.8 copy.13
  703.2 15.1 %all-to-all-done.1 = f32[32,128,64]{1,2,0:T(8,128)S(1)} async-done(((f32[32,128,64]{1,2,0:T(8,128)}), f32[32,128,64]{1,2,0:T(8,128)S(1)}, u32[]{:S(2)}, u32[]{:S(2)}) %all-to-all-start.1) | async-done | bytes 1048608 | tf_op jit(solution)/shard_map/all_to_all | solution.py:13
  718.3 0.3 fusion.4
  718.6 25.9 %psum.46 = f32[128,64]{0,1:T(8,128)S(1)} all-reduce(f32[128,64]{0,1:T(8,128)S(1)} %fusion.4), channel_id=1, replica_groups=mesh['samp'=32,'feat'=8] {'feat'}, use_global_device_ids=true, to_apply=%region_8.0 | all-reduce | flops 8192 | bytes 65536 | tf_op jit(solution)/shard_map/psum | solution.py:47
  744.7 110.7 %psum.47 = f32[64]{0:T(128)S(1)} all-reduce(f32[64]{0:T(128)S(1)} %multiply_reduce_fusion), channel_id=1, replica_groups=mesh['samp'=32,'feat'=8] {'samp'}, use_global_device_ids=true, to_apply=%region_10.0 | all-reduce | flops 64 | bytes 512 | tf_op jit(solution)/shard_map/psum | solution.py:48
  855.3 0.7 multiply_subtract_fusion
  (17 shorter events, 0.5 us)
Async XLA Ops:
  7.2 1.2 copy-start
  7.2 103.5 %all-gather.2.cloned.1.call-start = ((), (), s32[]{:S(2)}) async-start(), calls=%async_computation.3 | async-start | bytes 9437184 | tf_op jit(solution)/shard_map/all_gather | solution.py:22
  8.4 102.2 %copy-start.2 = (bf16[1024,64]{0,1:T(8,128)(2,1)S(1)}, bf16[1024,64]{0,1:T(8,128)(2,1)}, u32[]{:S(2)}) copy-start(bf16[1024,64]{0,1:T(8,128)(2,1)} %param.7) | copy-start | bytes 393220
  17.6 386.7 %reduce-scatter.2.cloned.1.call-start = ((), (), s32[]{:S(2)}) async-start(), calls=%async_computation.4 | async-start | bytes 9732096 | tf_op jit(solution)/shard_map/reduce_scatter | solution.py:25
  406.2 25.8 %copy-start.1 = (f32[128,576]{0,1:T(8,128)S(1)}, f32[128,576]{0,1:T(8,128)}, u32[]{:S(2)}) copy-start(f32[128,576]{0,1:T(8,128)} %reduce-scatter.2.cloned.1.call-done) | copy-start | bytes 884740
  406.2 25.8 %all-to-all-start = ((f32[32,128,64]{1,2,0:T(8,128)}), f32[32,128,64]{1,2,0:T(8,128)S(1)}, u32[]{:S(2)}, u32[]{:S(2)}) async-start(f32[32,128,64]{1,2,0:T(8,128)} %stack.4), calls=%async_computation.1 | async-start | bytes 2097152 | tf_op jit(solution)/shard_map/all_to_all | solution.py:13
  694.9 23.3 %all-to-all-start.1 = ((f32[32,128,64]{1,2,0:T(8,128)}), f32[32,128,64]{1,2,0:T(8,128)S(1)}, u32[]{:S(2)}, u32[]{:S(2)}) async-start(f32[32,128,64]{1,2,0:T(8,128)} %stack.5), calls=%async_computation.2 | async-start | bytes 2097152 | tf_op jit(solution)/shard_map/all_to_all | solution.py:13
Sparse Core Ops, SparseCore 0:
  17.8 92.8 all-gather.1
  120.7 283.5 reduce-scatter.1
